TPU v7x, 32 devices: a whole 2x2x4 slice. The times are simulated.
32 devices in a mesh: fsdp: 4 (over z), ctx: 8 (over y, x, core).
Axes of the slice: x: 2, y: 2, z: 4, core: 2. Of those that a mesh axis runs over, the one named last changes fastest.
Arguments:
- inputs: bfloat16 [24, 1024, 768], P('fsdp', 'ctx'), may hold values from -6 to 6
- cotangent: float32 [24, 1024, 768], P('fsdp', 'ctx'), may hold values from -6 to 6
- ln1_gain: bfloat16 [768], P(('fsdp', 'ctx')), may hold values from 0.5 to 1.5
- ln1_bias: bfloat16 [768], P(('fsdp', 'ctx')), may hold values from -1.25 to 1.25
- ln2_gain: bfloat16 [768], P(('fsdp', 'ctx')), may hold values from 0.5 to 1.5
- ln2_bias: bfloat16 [768], P(('fsdp', 'ctx')), may hold values from -1.25 to 1.25
- w_qkv: bfloat16 [768, 2304], P(('fsdp', 'ctx')), as said below
- b_qkv: bfloat16 [2304], P(('fsdp', 'ctx')), may hold values from -1.75 to 1.75
- w_out: bfloat16 [768, 768], P(('fsdp', 'ctx')), may hold values from -2.5 to 2.5
- b_out: bfloat16 [768], P(('fsdp', 'ctx')), may hold values from -1.75 to 1.75
- w_in: bfloat16 [768, 3072], P(('fsdp', 'ctx')), may hold values from -0.21875 to 0.21875
- b_in: bfloat16 [3072], P(('fsdp', 'ctx')), may hold values from -1.75 to 1.75
- w_mlp_out: bfloat16 [3072, 768], P(('fsdp', 'ctx')), may hold values from -0.109375 to 0.109375
- b_mlp_out: bfloat16 [768], P(('fsdp', 'ctx')), may hold values from -1.75 to 1.75
Outputs:
- outputs: float32 [24, 1024, 768], P('fsdp', 'ctx')
- grad_inputs: float32 [24, 1024, 768], P('fsdp', 'ctx')
- grad_ln1_gain: float32 [768], P(('fsdp', 'ctx'))
- grad_ln1_bias: float32 [768], P(('fsdp', 'ctx'))
- grad_ln2_gain: float32 [768], P(('fsdp', 'ctx'))
- grad_ln2_bias: float32 [768], P(('fsdp', 'ctx'))
- grad_w_qkv: float32 [768, 2304], P(('fsdp', 'ctx'))
- grad_b_qkv: float32 [2304], P(('fsdp', 'ctx'))
- grad_w_out: float32 [768, 768], P(('fsdp', 'ctx'))
- grad_b_out: float32 [768], P(('fsdp', 'ctx'))
- grad_w_in: float32 [768, 3072], P(('fsdp', 'ctx'))
- grad_b_in: float32 [3072], P(('fsdp', 'ctx'))
- grad_w_mlp_out: float32 [3072, 768], P(('fsdp', 'ctx'))
- grad_b_mlp_out: float32 [768], P(('fsdp', 'ctx'))
Inputs may be any that keep to these rules, and one draw needn't show every extreme that they name: `w_qkv`: a weight matrix whose entries lie within 24 / sqrt(768) of zero.
All inputs are finite; a program needn't handle non-finite values.
Results may differ from a plain program's by a relative error of at most 0.012.
Values may be sent and summed in bfloat16 or wider, within the bound.
No kernel may reach another device: no remote copies, remote signals or barrier semaphores. Data moves between devices by JAX's collectives and lax.ppermute only.
A program may use at most 448 MiB of HBM per device.

v0:
```python
import math
import jax
import jax.numpy as jnp
from jax import lax
from jax.sharding import PartitionSpec as P

HEADS = 12
HEAD_DIM = 64
ROT_DIM = 16
MICRO = 2
SEQ_MB = 3
EPS = 1e-05
BASE_FREQ = 10000.0


def layer_norm(values, gain_row, shift_row):
    centre = jnp.mean(values, axis=-1, keepdims=True)
    centred = values - centre
    inverse = lax.rsqrt(jnp.mean(centred * centred, axis=-1, keepdims=True) + EPS)
    normed = centred * inverse
    return (normed * gain_row + shift_row, normed, inverse)


def norm_back(grad_out, normed, inverse, gain_row):
    scaled = grad_out * gain_row
    return inverse * (
        scaled
        - jnp.mean(scaled, axis=-1, keepdims=True)
        - normed * jnp.mean(scaled * normed, axis=-1, keepdims=True)
    )


def angles(positions):
    half_rot = ROT_DIM // 2
    inv_freq = BASE_FREQ ** (-(2.0 * jnp.arange(half_rot, dtype=jnp.float32)) / ROT_DIM)
    phase_angle = positions.astype(jnp.float32)[:, None] * inv_freq[None, :]
    return (jnp.cos(phase_angle), jnp.sin(phase_angle))


def rotate(head_field, cosine, sine_rot, direction):
    half_rot = ROT_DIM // 2
    lead_half = head_field[..., :half_rot]
    trail_half = head_field[..., half_rot:ROT_DIM]
    cos_wide = cosine[:, None, :]
    sin_wide = direction * sine_rot[:, None, :]
    return jnp.concatenate(
        [
            lead_half * cos_wide - trail_half * sin_wide,
            trail_half * cos_wide + lead_half * sin_wide,
            head_field[..., ROT_DIM:],
        ],
        axis=-1,
    )


def gelu_parts(pre_act):
    normal_cdf = 0.5 * (1.0 + jax.scipy.special.erf(pre_act * 0.7071067811865476))
    density = jnp.exp(-0.5 * pre_act * pre_act) * 0.3989422804014327
    return (pre_act * normal_cdf, normal_cdf + pre_act * density)


def outer_rows(left, right):
    return lax.dot_general(
        left, right, (((0,), (0,)), ((), ())), preferred_element_type=jnp.float32
    )


def times_transpose(left, right):
    return lax.dot_general(
        left, right, (((1,), (1,)), ((), ())), preferred_element_type=jnp.float32
    )


def attend_block(soft_state, kv_block, first_row, query_low, positions, score_scale):
    run_max, run_sum, weighted = soft_state
    seq_count, block_rows, double_width = kv_block.shape
    model_width = double_width // 2
    key_low = kv_block[..., :model_width].reshape(seq_count, block_rows, HEADS, HEAD_DIM)
    value_low = kv_block[..., model_width:].reshape(seq_count, block_rows, HEADS, HEAD_DIM)
    scores = (
        jnp.einsum("sqhd,skhd->shqk", query_low, key_low, preferred_element_type=jnp.float32)
        * score_scale
    )
    allowed = (first_row + jnp.arange(block_rows, dtype=jnp.int32))[None, :] <= positions[:, None]
    scores = jnp.where(allowed, scores, -jnp.inf)
    new_max = jnp.maximum(run_max, jnp.max(scores, axis=-1))
    safe_max = jnp.where(new_max == -jnp.inf, 0.0, new_max)
    exp_scores = jnp.exp(scores - safe_max[..., None])
    factor = jnp.exp(run_max - safe_max)
    run_sum = run_sum * factor + jnp.sum(exp_scores, axis=-1)
    weighted = weighted * factor[..., None] + jnp.einsum(
        "shqk,skhd->shqd",
        exp_scores.astype(jnp.bfloat16),
        value_low,
        preferred_element_type=jnp.float32,
    )
    return (new_max, run_sum, weighted)


def attend_piece(soft_state, kv_piece, query_low, positions, score_scale):
    piece_rows = kv_piece.shape[1]
    step_rows = math.gcd(piece_rows, 512)

    def one_block(block_index, inner_state):
        offset = block_index * step_rows
        kv_block = lax.dynamic_slice_in_dim(kv_piece, offset, step_rows, 1)
        return attend_block(inner_state, kv_block, offset, query_low, positions, score_scale)

    return lax.fori_loop(0, piece_rows // step_rows, one_block, soft_state)


def local(
    inputs,
    cotangent,
    ln1_gain,
    ln1_bias,
    ln2_gain,
    ln2_bias,
    w_qkv,
    b_qkv,
    w_out,
    b_out,
    w_in,
    b_in,
    w_mlp_out,
    b_mlp_out,
):
    f32 = jnp.float32
    bf16 = jnp.bfloat16
    group_rows = inputs.shape[1]
    model_width = inputs.shape[2]
    seq_len = group_rows * lax.axis_size("ctx")
    key_block = math.gcd(seq_len, 512)
    score_scale = HEAD_DIM ** (-0.5)
    positions = lax.axis_index("ctx") * group_rows + jnp.arange(group_rows, dtype=jnp.int32)
    cosine, sine_rot = angles(positions)

    def gather_params():
        return (
            lax.all_gather(ln1_gain, ("fsdp", "ctx"), axis=0, tiled=True),
            lax.all_gather(ln1_bias, ("fsdp", "ctx"), axis=0, tiled=True),
            lax.all_gather(ln2_gain, ("fsdp", "ctx"), axis=0, tiled=True),
            lax.all_gather(ln2_bias, ("fsdp", "ctx"), axis=0, tiled=True),
            lax.all_gather(w_qkv, ("fsdp", "ctx"), axis=0, tiled=True),
            lax.all_gather(b_qkv, ("fsdp", "ctx"), axis=0, tiled=True),
            lax.all_gather(w_out, ("fsdp", "ctx"), axis=0, tiled=True),
            lax.all_gather(b_out, ("fsdp", "ctx"), axis=0, tiled=True),
            lax.all_gather(w_in, ("fsdp", "ctx"), axis=0, tiled=True),
            lax.all_gather(b_in, ("fsdp", "ctx"), axis=0, tiled=True),
            lax.all_gather(w_mlp_out, ("fsdp", "ctx"), axis=0, tiled=True),
            lax.all_gather(b_mlp_out, ("fsdp", "ctx"), axis=0, tiled=True),
        )

    weight_sums = None
    output_list = []
    grad_list = []
    for micro_index in range(MICRO):
        batch_rows = inputs[micro_index * SEQ_MB : (micro_index + 1) * SEQ_MB]
        cot_rows = cotangent[micro_index * SEQ_MB : (micro_index + 1) * SEQ_MB]
        seq_count = batch_rows.shape[0]
        flat_rows = seq_count * group_rows
        params_fwd = gather_params()
        (
            gain_one,
            shift_one,
            gain_two,
            shift_two,
            weight_qkv,
            bias_qkv,
            weight_out,
            bias_out,
            weight_in,
            bias_in,
            weight_mlp,
            bias_mlp,
        ) = params_fwd
        residual = batch_rows.reshape(flat_rows, model_width).astype(f32)
        normal_one, normed_one, inverse_one = layer_norm(
            residual, gain_one.astype(f32), shift_one.astype(f32)
        )
        normal_two, normed_two, inverse_two = layer_norm(
            residual, gain_two.astype(f32), shift_two.astype(f32)
        )
        hidden_one = normal_one.astype(bf16)
        hidden_two = normal_two.astype(bf16)
        project = jnp.dot(hidden_one, weight_qkv, preferred_element_type=f32) + bias_qkv.astype(f32)
        head_shape = (seq_count, group_rows, HEADS, HEAD_DIM)
        query_low = rotate(
            project[:, :model_width].reshape(head_shape), cosine, sine_rot, 1.0
        ).astype(bf16)
        key_low = rotate(
            project[:, model_width : 2 * model_width].reshape(head_shape), cosine, sine_rot, 1.0
        ).astype(bf16)
        value_low = project[:, 2 * model_width :].astype(bf16)
        kv_pack = jnp.concatenate(
            [
                key_low.reshape(seq_count, group_rows, model_width),
                value_low.reshape(seq_count, group_rows, model_width),
            ],
            axis=-1,
        )
        start_state = (
            jnp.full((seq_count, HEADS, group_rows), -jnp.inf, f32),
            jnp.zeros((seq_count, HEADS, group_rows), f32),
            jnp.zeros((seq_count, HEADS, group_rows, HEAD_DIM), f32),
        )
        soft_state = attend_piece(
            start_state,
            lax.all_gather(kv_pack, "ctx", axis=1, tiled=True),
            query_low,
            positions,
            score_scale,
        )
        run_max, run_sum, weighted = soft_state
        log_total = run_max + jnp.log(run_sum)
        attended = jnp.transpose(weighted / run_sum[..., None], (0, 2, 1, 3)).astype(bf16)
        att_flat = attended.reshape(flat_rows, model_width)
        pre_act = jnp.dot(hidden_two, weight_in, preferred_element_type=f32) + bias_in.astype(f32)
        activation_f, gelu_slope = gelu_parts(pre_act)
        activation = activation_f.astype(bf16)
        output = (
            residual
            + jnp.dot(att_flat, weight_out, preferred_element_type=f32)
            + bias_out.astype(f32)
            + jnp.dot(activation, weight_mlp, preferred_element_type=f32)
            + bias_mlp.astype(f32)
        )
        output_list.append(output.reshape(seq_count, group_rows, model_width))
        params_back = gather_params()
        (
            gain_one,
            shift_one,
            gain_two,
            shift_two,
            weight_qkv,
            bias_qkv,
            weight_out,
            bias_out,
            weight_in,
            bias_in,
            weight_mlp,
            bias_mlp,
        ) = params_back
        kv_rows = lax.all_gather(kv_pack, "ctx", axis=1, tiled=True)
        cot_flat = cot_rows.reshape(flat_rows, model_width)
        cot_low = cot_flat.astype(bf16)
        cot_sum = jnp.sum(cot_flat, axis=0)
        grad_w_out = outer_rows(att_flat, cot_low)
        grad_w_mlp = outer_rows(activation, cot_low)
        d_pre = times_transpose(cot_low, weight_mlp) * gelu_slope
        d_pre_low = d_pre.astype(bf16)
        grad_w_in = outer_rows(hidden_two, d_pre_low)
        d_hidden_two = times_transpose(d_pre_low, weight_in)
        grad_att = times_transpose(cot_low, weight_out).astype(bf16).reshape(head_shape)
        row_delta = jnp.einsum("sqhd,sqhd->shq", grad_att, attended, preferred_element_type=f32)

        def back_block(block_index, loop_carry):
            grad_query, buffer = loop_carry
            offset = block_index * key_block
            kv_block = lax.dynamic_slice_in_dim(kv_rows, offset, key_block, 1)
            key_part = kv_block[..., :model_width].reshape(seq_count, key_block, HEADS, HEAD_DIM)
            value_part = kv_block[..., model_width:].reshape(seq_count, key_block, HEADS, HEAD_DIM)
            scores = (
                jnp.einsum("sqhd,skhd->shqk", query_low, key_part, preferred_element_type=f32)
                * score_scale
            )
            allowed = (offset + jnp.arange(key_block, dtype=jnp.int32))[None, :] <= positions[
                :, None
            ]
            prob_block = jnp.where(allowed, jnp.exp(scores - log_total[..., None]), 0.0)
            grad_value = jnp.einsum(
                "shqk,sqhd->skhd", prob_block.astype(bf16), grad_att, preferred_element_type=f32
            )
            grad_prob = jnp.einsum(
                "sqhd,skhd->shqk", grad_att, value_part, preferred_element_type=f32
            )
            grad_score = (prob_block * (grad_prob - row_delta[..., None]) * score_scale).astype(
                bf16
            )
            grad_query = grad_query + jnp.einsum(
                "shqk,skhd->sqhd", grad_score, key_part, preferred_element_type=f32
            )
            grad_key = jnp.einsum(
                "shqk,sqhd->skhd", grad_score, query_low, preferred_element_type=f32
            )
            key_value_grad = jnp.concatenate(
                [
                    grad_key.reshape(seq_count, key_block, model_width),
                    grad_value.reshape(seq_count, key_block, model_width),
                ],
                axis=-1,
            )
            return (grad_query, lax.dynamic_update_slice_in_dim(buffer, key_value_grad, offset, 1))

        start_carry = (
            jnp.zeros(head_shape, f32),
            jnp.zeros((seq_count, seq_len, 2 * model_width), f32),
        )
        grad_query, buffer = lax.fori_loop(0, seq_len // key_block, back_block, start_carry)
        kv_grad_own = lax.psum_scatter(
            buffer.astype(jnp.bfloat16), "ctx", scatter_dimension=1, tiled=True
        ).astype(jnp.float32)
        key_grad_raw = kv_grad_own[..., :model_width].reshape(head_shape)
        value_grad_flat = kv_grad_own[..., model_width:].reshape(flat_rows, model_width)
        grad_query = rotate(grad_query, cosine, sine_rot, -1.0)
        grad_key = rotate(key_grad_raw, cosine, sine_rot, -1.0)
        d_project = jnp.concatenate(
            [
                grad_query.reshape(flat_rows, model_width),
                grad_key.reshape(flat_rows, model_width),
                value_grad_flat,
            ],
            axis=-1,
        )
        d_project_low = d_project.astype(bf16)
        grad_w_qkv = outer_rows(hidden_one, d_project_low)
        d_hidden_one = times_transpose(d_project_low, weight_qkv)
        grad_rows = (
            cot_flat
            + norm_back(d_hidden_one, normed_one, inverse_one, gain_one.astype(f32))
            + norm_back(d_hidden_two, normed_two, inverse_two, gain_two.astype(f32))
        )
        grad_list.append(grad_rows.reshape(seq_count, group_rows, model_width))
        terms = (
            jnp.sum(d_hidden_one * normed_one, axis=0),
            jnp.sum(d_hidden_one, axis=0),
            jnp.sum(d_hidden_two * normed_two, axis=0),
            jnp.sum(d_hidden_two, axis=0),
            grad_w_qkv,
            jnp.sum(d_project, axis=0),
            grad_w_out,
            cot_sum,
            grad_w_in,
            jnp.sum(d_pre, axis=0),
            grad_w_mlp,
            cot_sum,
        )
        if weight_sums is None:
            weight_sums = terms
        else:
            weight_sums = jax.tree.map(lambda total, term: total + term, weight_sums, terms)
    owned = (
        lax.psum_scatter(weight_sums[0], ("fsdp", "ctx"), scatter_dimension=0, tiled=True),
        lax.psum_scatter(weight_sums[1], ("fsdp", "ctx"), scatter_dimension=0, tiled=True),
        lax.psum_scatter(weight_sums[2], ("fsdp", "ctx"), scatter_dimension=0, tiled=True),
        lax.psum_scatter(weight_sums[3], ("fsdp", "ctx"), scatter_dimension=0, tiled=True),
        lax.psum_scatter(weight_sums[4], ("fsdp", "ctx"), scatter_dimension=0, tiled=True),
        lax.psum_scatter(weight_sums[5], ("fsdp", "ctx"), scatter_dimension=0, tiled=True),
        lax.psum_scatter(weight_sums[6], ("fsdp", "ctx"), scatter_dimension=0, tiled=True),
        lax.psum_scatter(weight_sums[7], ("fsdp", "ctx"), scatter_dimension=0, tiled=True),
        lax.psum_scatter(weight_sums[8], ("fsdp", "ctx"), scatter_dimension=0, tiled=True),
        lax.psum_scatter(weight_sums[9], ("fsdp", "ctx"), scatter_dimension=0, tiled=True),
        lax.psum_scatter(weight_sums[10], ("fsdp", "ctx"), scatter_dimension=0, tiled=True),
        lax.psum_scatter(weight_sums[11], ("fsdp", "ctx"), scatter_dimension=0, tiled=True),
    )
    outputs = jnp.concatenate(output_list, axis=0)
    grad_inputs = jnp.concatenate(grad_list, axis=0)
    return (
        outputs,
        grad_inputs,
        owned[0],
        owned[1],
        owned[2],
        owned[3],
        owned[4],
        owned[5],
        owned[6],
        owned[7],
        owned[8],
        owned[9],
        owned[10],
        owned[11],
    )


def solution(mesh):
    return jax.shard_map(
        local,
        mesh=mesh,
        in_specs=(
            P("fsdp", "ctx", None),
            P("fsdp", "ctx", None),
            P(("fsdp", "ctx")),
            P(("fsdp", "ctx")),
            P(("fsdp", "ctx")),
            P(("fsdp", "ctx")),
            P(("fsdp", "ctx"), None),
            P(("fsdp", "ctx")),
            P(("fsdp", "ctx"), None),
            P(("fsdp", "ctx")),
            P(("fsdp", "ctx"), None),
            P(("fsdp", "ctx")),
            P(("fsdp", "ctx"), None),
            P(("fsdp", "ctx")),
        ),
        out_specs=(
            P("fsdp", "ctx", None),
            P("fsdp", "ctx", None),
            P(("fsdp", "ctx")),
            P(("fsdp", "ctx")),
            P(("fsdp", "ctx")),
            P(("fsdp", "ctx")),
            P(("fsdp", "ctx"), None),
            P(("fsdp", "ctx")),
            P(("fsdp", "ctx"), None),
            P(("fsdp", "ctx")),
            P(("fsdp", "ctx"), None),
            P(("fsdp", "ctx")),
            P(("fsdp", "ctx"), None),
            P(("fsdp", "ctx")),
        ),
        check_vma=False,
    )
```

profile of v0, /device:TPU:0, one launch (start us, length us, event | category | flops | bytes accessed | tf_op | source)
XLA Modules:
  0.0 1064.9 jit_solution(9018735017955234770)
XLA Ops:
  15.5 42.9 %all-reduce.16 = (bf16[768]{0:T(1024)(128)(2,1)S(1)}, bf16[768]{0:T(1024)(128)(2,1)S(1)}, bf16[3072]{0:T(1024)(128)(2,1)}, bf16[768]{0:T(1024)(128)(2,1)}, bf16[...) all-reduce(bf16[768]{0:T(1024)(128)(2,1)S(1)} %dynamic-update-slice, ...), channel_id=1, replica_groups=mesh['fsdp'=4,'ctx'=8] {'fsdp','ctx'}, use_global_device_ids=true, to_apply=%add.5 | all-reduce | flops 9984 | bytes 39936
  64.4 9.1 all-gather.7.cloned.1.call-done
  108.7 20.5 %all-gather.11.cloned.1.call-done = bf16[768,768]{1,0:T(8,128)(2,1)} async-done(((bf16[24,768]{1,0:T(8,128)(2,1)}), bf16[768,768]{1,0:T(8,128)(2,1)}) %all-gather.11.cloned.1.call-update) | async-done | bytes 1179664 | tf_op jit(solution)/shard_map/all_gather | solution.py:146
  142.9 47.7 %all-gather.9.cloned.1.call-done = bf16[3,1024,1536]{1,2,0:T(8,128)(2,1)} async-done(((bf16[3,128,1536]{1,2,0:T(8,128)(2,1)}), bf16[3,1024,1536]{1,2,0:T(8,128)(2,1)}) %all-gather.9.cloned.1.call-update) | async-done | bytes 9437200 | tf_op jit(solution)/shard_map/all_gather | solution.py:209
  190.5 39.3 %while.68 = (s32[]{:T(128)}, f32[3,12,128]{2,1,0:T(8,128)S(1)}, f32[3,12,128]{2,1,0:T(8,128)S(1)}, f32[3,12,128,64]{2,3,1,0:T(8,128)}, bf16[3,1024,1536]{1,2,0:T...) while((s32[]{:T(128)}, f32[3,12,128]{2,1,0:T(8,128)S(1)}, ...), condition=%wide.region_5.0_spmd.clone, body=%wide.region_2.5_spmd.clone.sunk | while | flops 630924416 | bytes 83746024 | solution.py:109
  198.4 6.6 fusion.242
  217.3 5.9 fusion.242
  238.3 62.6 %while.70 = (s32[]{:T(128)}, f32[3,128,12,64]{1,3,2,0:T(8,128)}, bf16[3,1024,1536]{2,1,0:T(8,128)(2,1)}, bf16[3,1024,1536]{1,2,0:T(8,128)(2,1)}, bf16[3,128,12,6...) while((s32[]{:T(128)}, f32[3,128,12,64]{1,3,2,0:T(8,128)}, ...), condition=%wide.region_13.14_spmd.clone, body=%wide.region_12.13_spmd.clone.sunk | while | flops 1545994880 | bytes 116010296 | solution.py:299
  253.9 6.6 copy.224
  284.8 6.6 copy.224
  302.0 37.5 %while.69 = (s32[]{:T(128)}, f32[3,12,128]{2,1,0:T(8,128)S(1)}, f32[3,12,128]{2,1,0:T(8,128)S(1)}, f32[3,12,128,64]{2,3,1,0:T(8,128)}, bf16[3,1024,1536]{1,2,0:T...) while((s32[]{:T(128)}, f32[3,12,128]{2,1,0:T(8,128)S(1)}, ...), condition=%wide.region_11.12_spmd.clone, body=%wide.region_8.0_spmd.clone.sunk | while | flops 630924416 | bytes 83746024 | solution.py:109
  310.1 6.0 fusion.250
  328.1 5.9 fusion.250
  348.0 64.4 %while.71 = (s32[]{:T(128)}, f32[3,128,12,64]{1,3,2,0:T(8,128)}, bf16[3,1024,1536]{2,1,0:T(8,128)(2,1)}, bf16[3,1024,1536]{1,2,0:T(8,128)(2,1)}, bf16[3,128,12,6...) while((s32[]{:T(128)}, f32[3,128,12,64]{1,3,2,0:T(8,128)}, ...), condition=%wide.region_20.21_spmd.clone, body=%wide.region_19.20_spmd.clone.sunk | while | flops 1545994880 | bytes 116010296 | solution.py:299
  363.4 6.8 copy.225
  395.4 7.2 copy.225
  413.5 7.1 multiply_convert_fusion.1
  420.6 6.5 fusion.118
  470.4 72.2 %reduce-scatter.9.cloned.1.call-done = bf16[3,128,1536]{2,1,0:T(8,128)(2,1)} async-done(((bf16[3,1024,1536]{2,1,0:T(8,128)(2,1)}), bf16[3,128,1536]{2,1,0:T(8,128)(2,1)}) %reduce-scatter.9.cloned.1.call-update) | async-done | bytes 1179664 | tf_op jit(solution)/shard_map/reduce_scatter | solution.py:300
  601.6 42.3 %all-reduce.15 = (f32[768]{0:T(1024)S(1)}, f32[768]{0:T(1024)S(1)}, f32[768]{0:T(1024)S(1)}, f32[768]{0:T(1024)S(1)}, f32[2304]{0:T(1024)S(1)}, /*index=5*/f32[768]{0:T(1024)S(1)}, f32[3072]{0:T(1024)S(1)}) all-reduce(f32[768]{0:T(1024)S(1)} %add.485, f32[768]{0:T(1024)S(1)} %add.486, ...), channel_id=4, replica_groups=mesh['fsdp'=4,'ctx'=8] {'fsdp','ctx'}, use_global_device_ids=true, to_apply=%region_28.29.clone | all-reduce | flops 9216 | bytes 73728
  657.9 28.6 %reduce-scatter.15.cloned.1.call-done = f32[24,3072]{1,0:T(8,128)} async-done(((f32[768,3072]{1,0:T(8,128)}), f32[24,3072]{1,0:T(8,128)}) %reduce-scatter.15.cloned.1.call-update) | async-done | bytes 294928 | tf_op jit(solution)/shard_map/reduce_scatter | solution.py:351
  686.5 141.5 %reduce-scatter.17.cloned.1.call-done = f32[96,768]{1,0:T(8,128)} async-done(((f32[3072,768]{1,0:T(8,128)}), f32[96,768]{1,0:T(8,128)}) %reduce-scatter.17.cloned.1.call-update) | async-done | bytes 294928 | tf_op jit(solution)/shard_map/reduce_scatter | solution.py:353
  828.0 104.4 %reduce-scatter.13.cloned.1.call-done = f32[24,768]{1,0:T(8,128)} async-done(((f32[768,768]{1,0:T(8,128)}), f32[24,768]{1,0:T(8,128)}) %reduce-scatter.13.cloned.1.call-update) | async-done | bytes 73744 | tf_op jit(solution)/shard_map/reduce_scatter | solution.py:349
  932.3 124.8 %reduce-scatter.11.cloned.1.call-done = f32[24,2304]{1,0:T(8,128)} async-done(((f32[768,2304]{1,0:T(8,128)}), f32[24,2304]{1,0:T(8,128)}) %reduce-scatter.11.cloned.1.call-update) | async-done | bytes 221200 | tf_op jit(solution)/shard_map/reduce_scatter | solution.py:347
  (507 shorter events, 348.4 us)
Async XLA Ops:
  7.2 54.5 %copy-start.7 = (bf16[6,128,768]{2,1,0:T(8,128)(2,1)S(1)}, bf16[6,128,768]{2,1,0:T(8,128)(2,1)}, u32[]{:S(2)}) copy-start(bf16[6,128,768]{2,1,0:T(8,128)(2,1)} %param.22) | copy-start | bytes 3538948
  7.2 66.4 %all-gather.7.cloned.1.call-start = ((), (), s32[]{:S(2)}) async-start(), calls=%async_computation.6 | async-start | bytes 3649536 | tf_op jit(solution)/shard_map/all_gather | solution.py:144
  7.9 121.3 %all-gather.11.cloned.1.call-start = ((), (), s32[]{:S(2)}) async-start(), calls=%async_computation.8 | async-start | bytes 1216512 | tf_op jit(solution)/shard_map/all_gather | solution.py:146
  8.7 181.9 %all-gather.9.cloned.1.call-start = ((), (), s32[]{:S(2)}) async-start(), calls=%async_computation.7 | async-start | bytes 10616832 | tf_op jit(solution)/shard_map/all_gather | solution.py:209
  61.6 15.5 %copy-start.80 = (f32[384]{0:T(512)}, f32[384]{0:T(512)S(1)}, u32[]{:S(2)}) copy-start(f32[384]{0:T(512)S(1)} %rsqrt_bitcast_fusion) | copy-start | bytes 4612
  61.7 15.5 %copy-start.78 = (f32[384]{0:T(512)}, f32[384]{0:T(512)S(1)}, u32[]{:S(2)}) copy-start(f32[384]{0:T(512)S(1)} %rsqrt_bitcast_fusion.1) | copy-start | bytes 4612
  63.6 13.5 %copy-start.43 = (bf16[384,768]{1,0:T(8,128)(2,1)}, bf16[384,768]{1,0:T(8,128)(2,1)S(1)}, u32[]{:S(2)}) copy-start(bf16[384,768]{1,0:T(8,128)(2,1)S(1)} %get-tuple-element.948) | copy-start | bytes 1769476
  64.4 27.7 %copy-start.72 = (f32[128,8]{0,1:T(8,128)}, f32[128,8]{0,1:T(8,128)S(1)}, u32[]{:S(2)}) copy-start(f32[128,8]{0,1:T(8,128)S(1)} %get-tuple-element.973) | copy-start | bytes 12292
  96.9 204.1 %all-gather.17.cloned.1.call-start = ((), (), s32[]{:S(2)}) async-start(), calls=%async_computation.11 | async-start | bytes 10616832 | tf_op jit(solution)/shard_map/all_gather | solution.py:209
  103.9 309.1 %all-gather.13.cloned.1.call-start = ((), (), s32[]{:S(2)}) async-start(), calls=%async_computation.9 | async-start | bytes 4866048 | tf_op jit(solution)/shard_map/all_gather | solution.py:148
  104.5 316.1 %all-gather.15.cloned.1.call-start = ((), (), s32[]{:S(2)}) async-start(), calls=%async_computation.10 | async-start | bytes 4866048 | tf_op jit(solution)/shard_map/all_gather | solution.py:150
  105.1 362.0 %reduce-scatter.7.cloned.1.call-start = ((), (), s32[]{:S(2)}) async-start(), calls=%async_computation.12 | async-start | bytes 10616832 | tf_op jit(solution)/shard_map/reduce_scatter | solution.py:300
  108.7 22.5 %copy-start.45 = (bf16[384,768]{1,0:T(8,128)(2,1)}, bf16[384,768]{1,0:T(8,128)(2,1)S(1)}, u32[]{:S(2)}) copy-start(bf16[384,768]{1,0:T(8,128)(2,1)S(1)} %get-tuple-element.986) | copy-start | bytes 1769476
  301.0 241.6 %reduce-scatter.9.cloned.1.call-start = ((), (), s32[]{:S(2)}) async-start(), calls=%async_computation.13 | async-start | bytes 10616832 | tf_op jit(solution)/shard_map/reduce_scatter | solution.py:300
  412.4 274.1 %reduce-scatter.15.cloned.1.call-start = ((), (), s32[]{:S(2)}) async-start(), calls=%async_computation.16 | async-start | bytes 9732096 | tf_op jit(solution)/shard_map/reduce_scatter | solution.py:351
  433.6 15.1 %copy-start.23 = (bf16[384,3072]{1,0:T(8,128)(2,1)}, bf16[384,3072]{1,0:T(8,128)(2,1)S(1)}, u32[]{:S(2)}) copy-start(bf16[384,3072]{1,0:T(8,128)(2,1)S(1)} %get-tuple-element.974) | copy-start | bytes 7077892
  444.3 383.6 %reduce-scatter.17.cloned.1.call-start = ((), (), s32[]{:S(2)}) async-start(), calls=%async_computation.17 | async-start | bytes 9732096 | tf_op jit(solution)/shard_map/reduce_scatter | solution.py:353
  454.0 478.3 %reduce-scatter.13.cloned.1.call-start = ((), (), s32[]{:S(2)}) async-start(), calls=%async_computation.15 | async-start | bytes 2433024 | tf_op jit(solution)/shard_map/reduce_scatter | solution.py:349
  459.9 597.2 %reduce-scatter.11.cloned.1.call-start = ((), (), s32[]{:S(2)}) async-start(), calls=%async_computation.14 | async-start | bytes 7299072 | tf_op jit(solution)/shard_map/reduce_scatter | solution.py:347
  552.4 39.8 %copy-start.13 = (f32[96,8,3,128]{3,1,2,0:T(8,128)}, f32[96,8,3,128]{3,1,2,0:T(8,128)S(1)}, u32[]{:S(2)}) copy-start(f32[96,8,3,128]{3,1,2,0:T(8,128)S(1)} %copy.221) | copy-start | bytes 3538948
  580.4 16.4 %copy-start.55 = (f32[384,768]{1,0:T(8,128)}, f32[384,768]{1,0:T(8,128)S(1)}, u32[]{:S(2)}) copy-start(f32[384,768]{1,0:T(8,128)S(1)} %fusion.91) | copy-start | bytes 3538948
  582.8 14.0 %copy-start.57 = (f32[384,768]{1,0:T(8,128)}, f32[384,768]{1,0:T(8,128)S(1)}, u32[]{:S(2)}) copy-start(f32[384,768]{1,0:T(8,128)S(1)} %fusion.87) | copy-start | bytes 3538948
  596.9 55.9 %copy-start.12 = (f32[3,128,768]{2,1,0:T(8,128)S(1)}, f32[3,128,768]{2,1,0:T(8,128)}, u32[]{:S(2)}) copy-start(f32[3,128,768]{2,1,0:T(8,128)} %copy-done.11) | copy-start | bytes 3538948
  644.0 413.2 %copy-start.99 = (f32[24]{0:T(128)}, f32[24]{0:T(128)S(1)}, u32[]{:S(2)}) copy-start(f32[24]{0:T(128)S(1)} %dynamic-slice.5) | copy-start | bytes 292
  (102 other events, 289.2 us)
Sparse Core Ops, SparseCore 0:
  10.9 62.6 all-gather.6
  76.5 52.7 all-gather.10
  131.1 59.3 all-gather.8
  192.3 60.4 all-gather.16
  255.5 63.6 all-gather.12
  322.0 61.9 all-gather.14
  387.4 74.9 reduce-scatter.6
  465.9 76.6 reduce-scatter.8
  549.0 137.3 reduce-scatter.14
  692.8 135.1 reduce-scatter.16
  833.8 98.4 reduce-scatter.12
  938.4 118.6 reduce-scatter.10
where the time goes:
time: 1080 us; the launch traced here: 1060 us
  waiting for transfers between devices  551 us (51%)
  matrix products  170 us (16%)
  local copies, waits for them, and re-layouts  158 us (15%)
  blocking collectives  85.2 us (8%)
  other arithmetic  81.9 us (8%)
  between operations  16.1 us (1%)
    reduce_scatter x1, waiting for transfers between devices, local(): lax.psum_scatter(weight_sums[10], ('fsdp', 'ctx'), scatter_dimension=0, t...  141 us
    reduce_scatter x1, waiting for transfers between devices, local(): lax.psum_scatter(weight_sums[4], ('fsdp', 'ctx'), scatter_dimension=0, ti...  125 us
    reduce_scatter x1, waiting for transfers between devices, local(): lax.psum_scatter(weight_sums[6], ('fsdp', 'ctx'), scatter_dimension=0, ti...  104 us
    unnamed x2, blocking collectives  85.2 us
    reduce_scatter x2, waiting for transfers between devices, local(): lax.psum_scatter(buffer.astype(jnp.bfloat16), 'ctx', scatter_dimension=1,...  72.2 us
    all_gather x2, waiting for transfers between devices, local(): lax.all_gather(kv_pack, 'ctx', axis=1, tiled=True)  47.7 us
    dynamic_update_slice x8, local copies, waits for them, and re-layouts, back_block(): lax.dynamic_update_slice_in_dim(buffer, key_value_grad, offset, 1)  46.6 us
    unnamed x228, local copies, waits for them, and re-layouts  31.5 us
  transfers between devices with their start and end apart: 12, of which 8 were waited for; matrix products, arithmetic and copies ran while one was open for 37% of the time, Pallas kernels for 0%

commit v1 on v0

--- a/solution.py
+++ b/solution.py
@@ -1,3 +1,4 @@
+import functools
 import math
 import jax
 import jax.numpy as jnp
@@ -11,6 +12,15 @@
 SEQ_MB = 3
 EPS = 1e-05
 BASE_FREQ = 10000.0
+
+
+def things_draft(array_in, dimension_no):
+    r2 = lax.axis_size("ctx")
+    last = jnp.stack(r2 * [array_in])
+    return jnp.concatenate(lax.all_to_all(last, "ctx", 0, 0), dimension_no)
+
+
+draw_chunk_over_axis = functools.partial(things_draft, dimension_no=1)
 
 
 def layer_norm(values, gain_row, shift_row):
@@ -205,11 +215,7 @@
             jnp.zeros((seq_count, HEADS, group_rows, HEAD_DIM), f32),
         )
         soft_state = attend_piece(
-            start_state,
-            lax.all_gather(kv_pack, "ctx", axis=1, tiled=True),
-            query_low,
-            positions,
-            score_scale,
+            start_state, draw_chunk_over_axis(kv_pack), query_low, positions, score_scale
         )
         run_max, run_sum, weighted = soft_state
         log_total = run_max + jnp.log(run_sum)

time: 1080 us -> 1220 us (1.13)
  local copies, waits for them, and re-layouts: 158 us -> 219 us
  waiting for transfers between devices: 551 us -> 609 us
  matrix products: 170 us -> 190 us
    all_to_all x0 -> x2, waiting for transfers between devices: none -> 167 us  [things_draft(): return jnp.concatenate(lax.all_to_all(last, 'ctx', 0, 0), dimension_no)]
    reduce_scatter x1, waiting for transfers between devices: 28.6 us -> 134 us  [local(): lax.psum_scatter(weight_sums[8], ('fsdp', 'ctx'), scatter_dimension=0, ti...]
    reduce_scatter x1, waiting for transfers between devices: 104 us -> 0.01 us  [local(): lax.psum_scatter(weight_sums[6], ('fsdp', 'ctx'), scatter_dimension=0, ti...]
    all_gather x2, waiting for transfers between devices: 47.7 us -> 0.01 us  [local(): kv_rows = lax.all_gather(kv_pack, 'ctx', axis=1, tiled=True)]
    reduce_scatter x2, waiting for transfers between devices: 72.2 us -> 30.1 us  [local(): lax.psum_scatter(buffer.astype(jnp.bfloat16), 'ctx', scatter_dimension=1,...]
    all_to_all x0 -> x2, local copies, waits for them, and re-layouts: none -> 25.4 us  [things_draft(): return jnp.concatenate(lax.all_to_all(last, 'ctx', 0, 0), dimension_no)]
    all_gather x1, waiting for transfers between devices: 20.5 us -> 0.02 us  [gather_params(): lax.all_gather(w_out, ('fsdp', 'ctx'), axis=0, tiled=True)]
    while x36 -> x44, local copies, waits for them, and re-layouts: 5.05 us -> 23.3 us
  transfers between devices with their start and end apart: 12 -> 14, of which waited for: 8 -> 7; matrix products, arithmetic and copies ran while one was open for 37% -> 39% of each run, Pallas kernels for 0% -> 0%
where the time goes in v1:
time: 1220 us; the launch traced here: 1210 us
  waiting for transfers between devices  609 us (50%)
  local copies, waits for them, and re-layouts  219 us (18%)
  matrix products  190 us (16%)
  blocking collectives  83.6 us (7%)
  other arithmetic  79.5 us (7%)
  between operations  16.2 us (1%)
    all_to_all x2, waiting for transfers between devices, things_draft(): return jnp.concatenate(lax.all_to_all(last, 'ctx', 0, 0), dimension_no)  167 us
    reduce_scatter x1, waiting for transfers between devices, local(): lax.psum_scatter(weight_sums[10], ('fsdp', 'ctx'), scatter_dimension=0, t...  142 us
    reduce_scatter x1, waiting for transfers between devices, local(): lax.psum_scatter(weight_sums[8], ('fsdp', 'ctx'), scatter_dimension=0, ti...  134 us
    reduce_scatter x1, waiting for transfers between devices, local(): lax.psum_scatter(weight_sums[4], ('fsdp', 'ctx'), scatter_dimension=0, ti...  125 us
    unnamed x2, blocking collectives  83.6 us
    dynamic_update_slice x8, local copies, waits for them, and re-layouts, back_block(): lax.dynamic_update_slice_in_dim(buffer, key_value_grad, offset, 1)  46.2 us
    dot_general x4, matrix products, attend_block(): jnp.einsum('shqk,skhd->shqd', exp_scores.astype(jnp.bfloat16), value_low,...  33 us
    unnamed x222, local copies, waits for them, and re-layouts  30.5 us
  transfers between devices with their start and end apart: 14, of which 7 were waited for; matrix products, arithmetic and copies ran while one was open for 39% of the time, Pallas kernels for 0%

profile of v1, /device:TPU:0, one launch (start us, length us, event | category | flops | bytes accessed | tf_op | source)
XLA Modules:
  0.0 1209.7 jit_solution(384002076512534675)
XLA Ops:
  15.5 42.9 %all-reduce.16 = (bf16[768]{0:T(1024)(128)(2,1)S(1)}, bf16[768]{0:T(1024)(128)(2,1)S(1)}, bf16[3072]{0:T(1024)(128)(2,1)}, bf16[768]{0:T(1024)(128)(2,1)}, bf16[...) all-reduce(bf16[768]{0:T(1024)(128)(2,1)S(1)} %dynamic-update-slice, ...), channel_id=1, replica_groups=mesh['fsdp'=4,'ctx'=8] {'fsdp','ctx'}, use_global_device_ids=true, to_apply=%add.5 | all-reduce | flops 9984 | bytes 39936
  64.4 9.2 all-gather.7.cloned.1.call-done
  116.7 125.5 %all-to-all-done = bf16[8,3,128,1536]{2,3,1,0:T(8,128)(2,1)} async-done(((bf16[8,3,128,1536]{2,3,1,0:T(8,128)(2,1)}), bf16[8,3,128,1536]{2,3,1,0:T(8,128)(2,1)}, u32[]{:S(2)}, u32[]{:S(2)}) %all-to-all-start) | async-done | bytes 9437216 | tf_op jit(solution)/shard_map/all_to_all | solution.py:20
  267.5 12.7 %copy.151 = bf16[8,3,128,1536]{3,2,0,1:T(8,128)(2,1)} copy(bf16[8,3,128,1536]{2,3,1,0:T(8,128)(2,1)} %all-to-all-done) | data formatting | bytes 18874368 | tf_op jit(solution)/shard_map/all_to_all | solution.py:20
  280.2 59.0 %while.68 = (s32[]{:T(128)}, f32[3,12,128]{2,1,0:T(8,128)S(1)}, f32[3,12,128]{2,1,0:T(8,128)S(1)}, f32[3,12,128,64]{2,3,1,0:T(8,128)}, bf16[3,1024,1536]{2,1,0:T...) while((s32[]{:T(128)}, f32[3,12,128]{2,1,0:T(8,128)S(1)}, ...), condition=%wide.region_5.0_spmd.clone, body=%wide.region_2.5_spmd.clone.sunk | while | flops 630924416 | bytes 64871652 | solution.py:119
  301.8 8.1 fusion.244
  330.8 8.4 fusion.244
  343.2 41.5 %all-to-all-done.1 = bf16[8,3,128,1536]{2,3,1,0:T(8,128)(2,1)} async-done(((bf16[8,3,128,1536]{2,3,1,0:T(8,128)(2,1)}), bf16[8,3,128,1536]{2,3,1,0:T(8,128)(2,1)}, u32[]{:S(2)}, u32[]{:S(2)}) %all-to-all-start.1) | async-done | bytes 9437216 | tf_op jit(solution)/shard_map/all_to_all | solution.py:20
  384.8 12.7 %copy.159 = bf16[8,3,128,1536]{3,2,0,1:T(8,128)(2,1)} copy(bf16[8,3,128,1536]{2,3,1,0:T(8,128)(2,1)} %all-to-all-done.1) | data formatting | bytes 18874368 | tf_op jit(solution)/shard_map/all_to_all | solution.py:20
  401.9 62.5 %while.70 = (s32[]{:T(128)}, f32[3,128,12,64]{1,3,2,0:T(8,128)}, bf16[3,1024,1536]{2,1,0:T(8,128)(2,1)}, bf16[3,1024,1536]{1,2,0:T(8,128)(2,1)}, bf16[3,128,12,6...) while((s32[]{:T(128)}, f32[3,128,12,64]{1,3,2,0:T(8,128)}, ...), condition=%wide.region_13.14_spmd.clone, body=%wide.region_12.13_spmd.clone.sunk | while | flops 1545994880 | bytes 116010296 | solution.py:305
  417.2 6.7 copy.284
  448.1 6.7 copy.284
  465.5 59.5 %while.69 = (s32[]{:T(128)}, f32[3,12,128]{2,1,0:T(8,128)S(1)}, f32[3,12,128]{2,1,0:T(8,128)S(1)}, f32[3,12,128,64]{2,3,1,0:T(8,128)}, bf16[3,1024,1536]{2,1,0:T...) while((s32[]{:T(128)}, f32[3,12,128]{2,1,0:T(8,128)S(1)}, ...), condition=%wide.region_11.12_spmd.clone, body=%wide.region_8.0_spmd.clone.sunk | while | flops 630924416 | bytes 64871652 | solution.py:119
  486.7 8.1 fusion.252
  516.5 8.5 fusion.252
  533.3 63.8 %while.71 = (s32[]{:T(128)}, f32[3,128,12,64]{1,3,2,0:T(8,128)}, bf16[3,1024,1536]{2,1,0:T(8,128)(2,1)}, bf16[3,1024,1536]{1,2,0:T(8,128)(2,1)}, bf16[3,128,12,6...) while((s32[]{:T(128)}, f32[3,128,12,64]{1,3,2,0:T(8,128)}, ...), condition=%wide.region_20.21_spmd.clone, body=%wide.region_19.20_spmd.clone.sunk | while | flops 1545994880 | bytes 116010296 | solution.py:305
  549.2 6.7 copy.285
  580.7 6.7 copy.285
  599.7 7.2 multiply_convert_fusion.1
  658.5 30.1 %reduce-scatter.9.cloned.1.call-done = bf16[3,128,1536]{2,1,0:T(8,128)(2,1)} async-done(((bf16[3,1024,1536]{2,1,0:T(8,128)(2,1)}), bf16[3,128,1536]{2,1,0:T(8,128)(2,1)}) %reduce-scatter.9.cloned.1.call-update) | async-done | bytes 1179664 | tf_op jit(solution)/shard_map/reduce_scatter | solution.py:306
  746.9 40.7 %all-reduce.15 = (f32[768]{0:T(1024)S(1)}, f32[768]{0:T(1024)S(1)}, f32[768]{0:T(1024)S(1)}, f32[768]{0:T(1024)S(1)}, f32[2304]{0:T(1024)S(1)}, /*index=5*/f32[768]{0:T(1024)S(1)}, f32[3072]{0:T(1024)S(1)}) all-reduce(f32[768]{0:T(1024)S(1)} %add.485, f32[768]{0:T(1024)S(1)} %add.486, ...), channel_id=4, replica_groups=mesh['fsdp'=4,'ctx'=8] {'fsdp','ctx'}, use_global_device_ids=true, to_apply=%region_28.29.clone | all-reduce | flops 9216 | bytes 73728
  801.6 134.0 %reduce-scatter.15.cloned.1.call-done = f32[24,3072]{1,0:T(8,128)} async-done(((f32[768,3072]{1,0:T(8,128)}), f32[24,3072]{1,0:T(8,128)}) %reduce-scatter.15.cloned.1.call-update) | async-done | bytes 294928 | tf_op jit(solution)/shard_map/reduce_scatter | solution.py:357
  935.6 141.6 %reduce-scatter.17.cloned.1.call-done = f32[96,768]{1,0:T(8,128)} async-done(((f32[3072,768]{1,0:T(8,128)}), f32[96,768]{1,0:T(8,128)}) %reduce-scatter.17.cloned.1.call-update) | async-done | bytes 294928 | tf_op jit(solution)/shard_map/reduce_scatter | solution.py:359
  1077.2 124.6 %reduce-scatter.11.cloned.1.call-done = f32[24,2304]{1,0:T(8,128)} async-done(((f32[768,2304]{1,0:T(8,128)}), f32[24,2304]{1,0:T(8,128)}) %reduce-scatter.11.cloned.1.call-update) | async-done | bytes 221200 | tf_op jit(solution)/shard_map/reduce_scatter | solution.py:353
  (517 shorter events, 409.8 us)
Async XLA Ops:
  7.2 54.5 %copy-start.7 = (bf16[6,128,768]{2,1,0:T(8,128)(2,1)S(1)}, bf16[6,128,768]{2,1,0:T(8,128)(2,1)}, u32[]{:S(2)}) copy-start(bf16[6,128,768]{2,1,0:T(8,128)(2,1)} %param.22) | copy-start | bytes 3538948
  7.2 66.4 %all-gather.7.cloned.1.call-start = ((), (), s32[]{:S(2)}) async-start(), calls=%async_computation.8 | async-start | bytes 3649536 | tf_op jit(solution)/shard_map/all_gather | solution.py:154
  7.9 245.1 %all-gather.9.cloned.1.call-start = ((), (), s32[]{:S(2)}) async-start(), calls=%async_computation.9 | async-start | bytes 1216512 | tf_op jit(solution)/shard_map/all_gather | solution.py:156
  8.7 388.8 %all-gather.15.cloned.1.call-start = ((), (), s32[]{:S(2)}) async-start(), calls=%async_computation.12 | async-start | bytes 10616832 | tf_op jit(solution)/shard_map/all_gather | solution.py:250
  61.6 15.5 %copy-start.78 = (f32[384]{0:T(512)}, f32[384]{0:T(512)S(1)}, u32[]{:S(2)}) copy-start(f32[384]{0:T(512)S(1)} %rsqrt_bitcast_fusion) | copy-start | bytes 4612
  64.4 27.7 %copy-start.70 = (f32[128,8]{0,1:T(8,128)}, f32[128,8]{0,1:T(8,128)S(1)}, u32[]{:S(2)}) copy-start(f32[128,8]{0,1:T(8,128)S(1)} %get-tuple-element.1005) | copy-start | bytes 12292
  96.2 432.8 %all-gather.17.cloned.1.call-start = ((), (), s32[]{:S(2)}) async-start(), calls=%async_computation.14 | async-start | bytes 10616832 | tf_op jit(solution)/shard_map/all_gather | solution.py:250
  101.4 498.3 %all-gather.11.cloned.1.call-start = ((), (), s32[]{:S(2)}) async-start(), calls=%async_computation.10 | async-start | bytes 4866048 | tf_op jit(solution)/shard_map/all_gather | solution.py:158
  107.7 134.6 %all-to-all-start = ((bf16[8,3,128,1536]{2,3,1,0:T(8,128)(2,1)}), bf16[8,3,128,1536]{2,3,1,0:T(8,128)(2,1)}, u32[]{:S(2)}, u32[]{:S(2)}) async-start(bf16[8,3,128,1536]{2,3,1,0:T(8,128)(2,1)} %stack.4), calls=%async_computation | async-start | bytes 18874368 | tf_op jit(solution)/shard_map/all_to_all | solution.py:20
  112.8 498.4 %all-gather.13.cloned.1.call-start = ((), (), s32[]{:S(2)}) async-start(), calls=%async_computation.11 | async-start | bytes 4866048 | tf_op jit(solution)/shard_map/all_gather | solution.py:160
  114.3 127.9 %copy-start.13 = (bf16[3,128,1536]{1,2,0:T(8,128)(2,1)S(1)}, bf16[3,128,1536]{1,2,0:T(8,128)(2,1)}, u32[]{:S(2)}) copy-start(bf16[3,128,1536]{1,2,0:T(8,128)(2,1)} %pad_maximum_fusion.9) | copy-start | bytes 3538948
  116.7 136.3 %copy-start.47 = (bf16[384,768]{1,0:T(8,128)(2,1)}, bf16[384,768]{1,0:T(8,128)(2,1)S(1)}, u32[]{:S(2)}) copy-start(bf16[384,768]{1,0:T(8,128)(2,1)S(1)} %get-tuple-element.1018) | copy-start | bytes 1769476
  247.8 136.9 %all-to-all-start.1 = ((bf16[8,3,128,1536]{2,3,1,0:T(8,128)(2,1)}), bf16[8,3,128,1536]{2,3,1,0:T(8,128)(2,1)}, u32[]{:S(2)}, u32[]{:S(2)}) async-start(bf16[8,3,128,1536]{2,3,1,0:T(8,128)(2,1)} %stack.5), calls=%async_computation.1 | async-start | bytes 18874368 | tf_op jit(solution)/shard_map/all_to_all | solution.py:20
  253.0 402.3 %reduce-scatter.7.cloned.1.call-start = ((), (), s32[]{:S(2)}) async-start(), calls=%async_computation.13 | async-start | bytes 10616832 | tf_op jit(solution)/shard_map/reduce_scatter | solution.py:306
  464.4 224.1 %reduce-scatter.9.cloned.1.call-start = ((), (), s32[]{:S(2)}) async-start(), calls=%async_computation.15 | async-start | bytes 10616832 | tf_op jit(solution)/shard_map/reduce_scatter | solution.py:306
  597.2 204.4 %reduce-scatter.13.cloned.1.call-start = ((), (), s32[]{:S(2)}) async-start(), calls=%async_computation.17 | async-start | bytes 2433024 | tf_op jit(solution)/shard_map/reduce_scatter | solution.py:355
  611.1 324.5 %reduce-scatter.15.cloned.1.call-start = ((), (), s32[]{:S(2)}) async-start(), calls=%async_computation.18 | async-start | bytes 9732096 | tf_op jit(solution)/shard_map/reduce_scatter | solution.py:357
  627.1 15.5 %copy-start.25 = (bf16[384,3072]{1,0:T(8,128)(2,1)}, bf16[384,3072]{1,0:T(8,128)(2,1)S(1)}, u32[]{:S(2)}) copy-start(bf16[384,3072]{1,0:T(8,128)(2,1)S(1)} %get-tuple-element.1006) | copy-start | bytes 7077892
  638.0 439.3 %reduce-scatter.17.cloned.1.call-start = ((), (), s32[]{:S(2)}) async-start(), calls=%async_computation.19 | async-start | bytes 9732096 | tf_op jit(solution)/shard_map/reduce_scatter | solution.py:359
  647.9 554.0 %reduce-scatter.11.cloned.1.call-start = ((), (), s32[]{:S(2)}) async-start(), calls=%async_computation.16 | async-start | bytes 7299072 | tf_op jit(solution)/shard_map/reduce_scatter | solution.py:353
  698.5 39.0 %copy-start.15 = (f32[96,8,3,128]{3,1,2,0:T(8,128)}, f32[96,8,3,128]{3,1,2,0:T(8,128)S(1)}, u32[]{:S(2)}) copy-start(f32[96,8,3,128]{3,1,2,0:T(8,128)S(1)} %copy.273) | copy-start | bytes 3538948
  725.9 16.2 %copy-start.57 = (f32[384,768]{1,0:T(8,128)}, f32[384,768]{1,0:T(8,128)S(1)}, u32[]{:S(2)}) copy-start(f32[384,768]{1,0:T(8,128)S(1)} %fusion.91) | copy-start | bytes 3538948
  742.2 54.4 %copy-start.12 = (f32[3,128,768]{2,1,0:T(8,128)S(1)}, f32[3,128,768]{2,1,0:T(8,128)}, u32[]{:S(2)}) copy-start(f32[3,128,768]{2,1,0:T(8,128)} %copy-done.11) | copy-start | bytes 3538948
  787.7 414.2 %copy-start.96 = (f32[24]{0:T(128)}, f32[24]{0:T(128)S(1)}, u32[]{:S(2)}) copy-start(f32[24]{0:T(128)S(1)} %dynamic-slice.5) | copy-start | bytes 292
  (101 other events, 326.9 us)
Sparse Core Ops, SparseCore 0:
  10.9 62.6 all-gather.6
  76.5 54.0 all-gather.8
  132.4 131.1 all-gather.14
  265.4 135.6 all-gather.16
  403.8 61.3 all-gather.10
  468.0 61.9 all-gather.12
  533.4 74.9 reduce-scatter.6
  611.9 76.6 reduce-scatter.8
  694.4 99.5 reduce-scatter.12
  800.4 135.1 reduce-scatter.14
  942.1 135.1 reduce-scatter.16
  1083.3 118.4 reduce-scatter.10
